TPU v7x, 32 devices: a whole 2x2x4 slice. The times are simulated.
32 devices in a mesh: outer: 8 (over z, x), inner: 4 (over y, core).
Axes of the slice: x: 2, y: 2, z: 4, core: 2. Of those that a mesh axis runs over, the one named last changes fastest.
Arguments:
- inputs: bfloat16 [16384, 512], P(('outer', 'inner')), may hold values from -6 to 6
- weights: bfloat16 [3151872], replicated
- cotangent: bfloat16 [16384, 512], P(('outer', 'inner')), may hold values from -6 to 6
- clip_lengths: int32 [11], replicated, may hold values from 1 to 1500, 16384 in all
- first_moment: float32 [3151872], P('inner')
- second_moment: float32 [3151872], P('inner')
Outputs:
- layer_output: bfloat16 [16384, 512], P(('outer', 'inner'))
- input_grad: bfloat16 [16384, 512], P(('outer', 'inner'))
- weight_grads: float32 [3151872], P('inner')
- grad_norm: float32 [], replicated
- moment_one: float32 [3151872], P('inner')
- moment_two: float32 [3151872], P('inner')
- weight_step: bfloat16 [3151872], replicated
Inputs may be any that keep to these rules, and one draw needn't show every extreme that they name: `clip_lengths`: the lengths add up to 16384; clip c occupies the slots from the sum of the lengths before it on, in order.
All inputs are finite; a program needn't handle non-finite values.
Results may differ from a plain program's by a relative error of at most 0.015.
Values may be sent and summed in bfloat16 or wider, within the bound.
No kernel may reach another device: no remote copies, remote signals or barrier semaphores. Data moves between devices by JAX's collectives and lax.ppermute only.
A program may use at most 192 MiB of HBM per device.

v0:
```python
import math
import jax
import jax.numpy as jnp
from jax import lax
from jax.sharding import PartitionSpec as P

D = 512
HEADS = 8
FF = 2048
MOST = 1500
BETA_ONE = 0.9
BETA_TWO = 0.999
FIX_ONE = 1.0 - (0.9**10) ** 10
FIX_TWO = 1.0 - (0.999**10) ** 10
DECAY = 0.1
INV_ROOT_TWO = 1.0 / math.sqrt(2.0)
INV_ROOT_TWO_PI = 1.0 / math.sqrt(2.0 * math.pi)


def passed_along(block, axis, distance):
    devices = range(lax.axis_size(axis))
    route = [(i - distance, i) for i in devices if i - distance in devices]
    return lax.ppermute(block, axis, route)


def layouts():
    return [
        (D,),
        (D,),
        (D, D),
        (D,),
        (D, D),
        (D, D),
        (D,),
        (D, D),
        (D,),
        (D,),
        (D,),
        (D, FF),
        (FF,),
        (FF, D),
        (D,),
    ]


def unpack(flat):
    sections = []
    offset = 0
    for layout in layouts():
        entries = 1
        for extent in layout:
            entries = entries * extent
        section = flat[offset : offset + entries].reshape(layout)
        if len(layout) == 1:
            section = section.astype(jnp.float32)
        sections.append(section)
        offset = offset + entries
    return sections


def plain_dot(matrix_one, matrix_two):
    return jnp.dot(matrix_one, matrix_two, preferred_element_type=jnp.float32)


def rows_dot(matrix_one, matrix_two):
    return lax.dot_general(
        matrix_one, matrix_two, (((0,), (0,)), ((), ())), preferred_element_type=jnp.float32
    )


def back_dot(matrix_one, matrix_two):
    return lax.dot_general(
        matrix_one, matrix_two, (((1,), (1,)), ((), ())), preferred_element_type=jnp.float32
    )


def standard(values):
    center = jnp.mean(values, axis=-1, keepdims=True)
    centered = values - center
    inverse_dev = lax.rsqrt(jnp.mean(centered * centered, axis=-1, keepdims=True) + 1e-05)
    return (centered * inverse_dev, inverse_dev)


def norm_back(grad_normed, normed_hat, inverse_dev, gain):
    scaled = grad_normed * gain
    return inverse_dev * (
        scaled
        - jnp.mean(scaled, axis=-1, keepdims=True)
        - normed_hat * jnp.mean(scaled * normed_hat, axis=-1, keepdims=True)
    )


def bounds(positions, clip_lengths):
    starts = jnp.cumsum(clip_lengths, dtype=jnp.int32) - clip_lengths
    member = (
        jnp.sum((positions[:, None] >= starts[None, :]).astype(jnp.int32), axis=1, dtype=jnp.int32)
        - 1
    )
    onehot = (
        jnp.arange(clip_lengths.shape[0], dtype=jnp.int32)[None, :] == member[:, None]
    ).astype(jnp.int32)
    lower_slot = jnp.sum(onehot * starts[None, :], axis=1, dtype=jnp.int32)
    upper_slot = lower_slot + jnp.sum(onehot * clip_lengths[None, :], axis=1, dtype=jnp.int32)
    return (lower_slot, upper_slot)


def fetch_keys(pair, distance):
    return passed_along((pair[0], pair[1]), ("outer", "inner"), -distance)


def return_grads(pair, distance):
    return (
        passed_along(pair[0].astype(jnp.bfloat16), ("outer", "inner"), distance).astype(
            jnp.float32
        ),
        passed_along(pair[1].astype(jnp.bfloat16), ("outer", "inner"), distance).astype(
            jnp.float32
        ),
    )


def on_device(inputs, weights, cotangent, clip_lengths, first_moment, second_moment):
    tok_rows = inputs.shape[0]
    reach = (MOST + tok_rows - 2) // tok_rows
    head_width = D // HEADS
    score_scale = 1.0 / math.sqrt(head_width)
    (
        first_gain,
        first_bias,
        query_weight,
        query_bias,
        key_weight,
        value_weight,
        value_bias,
        out_weight,
        out_bias,
        second_gain,
        second_bias,
        up_weight,
        up_bias,
        down_weight,
        down_bias,
    ) = unpack(weights)
    base_slot = lax.axis_index(("outer", "inner")) * tok_rows
    positions = base_slot + jnp.arange(tok_rows, dtype=jnp.int32)
    lower_slot, upper_slot = bounds(positions, clip_lengths)
    input_rows = inputs.astype(jnp.float32)
    first_hat, first_dev = standard(input_rows)
    normed = (first_hat * first_gain + first_bias).astype(jnp.bfloat16)
    query_rows = (plain_dot(normed, query_weight) + query_bias).astype(jnp.bfloat16)
    key_rows = plain_dot(normed, key_weight).astype(jnp.bfloat16)
    value_rows = (plain_dot(normed, value_weight) + value_bias).astype(jnp.bfloat16)
    distances = list(range(-reach, reach + 1))
    key_list = []
    value_list = []
    for distance in distances:
        if distance == 0:
            pair = (key_rows, value_rows)
        else:
            pair = fetch_keys((key_rows, value_rows), distance)
        key_list.append(pair[0])
        value_list.append(pair[1])
    block_count = len(distances)
    key_stack = jnp.stack(key_list).reshape(block_count, tok_rows, HEADS, head_width)
    value_stack = jnp.stack(value_list).reshape(block_count, tok_rows, HEADS, head_width)
    block_shift = jnp.arange(-reach, reach + 1, dtype=jnp.int32)
    query_heads = query_rows.reshape(tok_rows, HEADS, head_width)

    def block_scores(key_block, shift_block):
        places = base_slot + shift_block * tok_rows + jnp.arange(tok_rows, dtype=jnp.int32)
        allowed = (places[None, :] >= lower_slot[:, None]) & (places[None, :] < upper_slot[:, None])
        raw_scores = jnp.einsum(
            "qhd,khd->hqk", query_heads, key_block, preferred_element_type=jnp.float32
        )
        return jnp.where(allowed[None], score_scale * raw_scores, -1e30)

    def first_pass(carried, block_data):
        row_peak, row_total = carried
        key_block, shift_block = block_data
        scores = block_scores(key_block, shift_block)
        new_peak = jnp.maximum(row_peak, jnp.max(scores, axis=-1))
        row_total = row_total * jnp.exp(row_peak - new_peak) + jnp.sum(
            jnp.exp(scores - new_peak[:, :, None]), axis=-1
        )
        return ((new_peak, row_total), None)

    start_peak = jnp.full((HEADS, tok_rows), -1e30, jnp.float32)
    start_total = jnp.zeros((HEADS, tok_rows), jnp.float32)
    (row_peak, row_total), _ = lax.scan(
        first_pass, (start_peak, start_total), (key_stack, block_shift)
    )
    log_total = row_peak + jnp.log(row_total)

    def second_pass(carried, block_data):
        key_block, value_block, shift_block = block_data
        soft_weights = jnp.exp(block_scores(key_block, shift_block) - log_total[:, :, None])
        return (
            carried
            + jnp.einsum(
                "hqk,khd->qhd",
                soft_weights.astype(jnp.bfloat16),
                value_block,
                preferred_element_type=jnp.float32,
            ),
            None,
        )

    attended, _ = lax.scan(
        second_pass,
        jnp.zeros((tok_rows, HEADS, head_width), jnp.float32),
        (key_stack, value_stack, block_shift),
    )
    mixed = attended.reshape(tok_rows, D).astype(jnp.bfloat16)
    middle = input_rows + plain_dot(mixed, out_weight) + out_bias
    second_hat, second_dev = standard(middle)
    hidden_in = (second_hat * second_gain + second_bias).astype(jnp.bfloat16)
    up_rows = plain_dot(hidden_in, up_weight) + up_bias
    cdf_part = 0.5 * (1.0 + lax.erf(up_rows * INV_ROOT_TWO))
    activated = (up_rows * cdf_part).astype(jnp.bfloat16)
    layer_output = (middle + plain_dot(activated, down_weight) + down_bias).astype(jnp.bfloat16)
    grad_out = cotangent.astype(jnp.float32)
    down_grad = rows_dot(activated, cotangent)
    down_bias_grad = jnp.sum(grad_out, axis=0)
    grad_act = back_dot(cotangent, down_weight)
    pdf_part = jnp.exp(-0.5 * up_rows * up_rows) * INV_ROOT_TWO_PI
    grad_up = (grad_act * (cdf_part + up_rows * pdf_part)).astype(jnp.bfloat16)
    up_grad = rows_dot(hidden_in, grad_up)
    up_bias_grad = jnp.sum(grad_up.astype(jnp.float32), axis=0)
    grad_hidden = back_dot(grad_up, up_weight)
    second_gain_grad = jnp.sum(grad_hidden * second_hat, axis=0)
    second_bias_grad = jnp.sum(grad_hidden, axis=0)
    grad_middle = grad_out + norm_back(grad_hidden, second_hat, second_dev, second_gain)
    grad_branch = grad_middle.astype(jnp.bfloat16)
    out_grad = rows_dot(mixed, grad_branch)
    out_bias_grad = jnp.sum(grad_branch.astype(jnp.float32), axis=0)
    grad_mixed = back_dot(grad_branch, out_weight).astype(jnp.bfloat16)
    grad_heads = grad_mixed.reshape(tok_rows, HEADS, head_width)
    row_delta = jnp.sum(grad_heads.astype(jnp.float32) * attended, axis=-1).T

    def back_pass(grad_query, block_data):
        key_block, value_block, shift_block = block_data
        soft_weights = jnp.exp(block_scores(key_block, shift_block) - log_total[:, :, None])
        grad_probs = jnp.einsum(
            "qhd,khd->hqk", grad_heads, value_block, preferred_element_type=jnp.float32
        )
        grad_scores = (score_scale * soft_weights * (grad_probs - row_delta[:, :, None])).astype(
            jnp.bfloat16
        )
        value_part = jnp.einsum(
            "hqk,qhd->khd",
            soft_weights.astype(jnp.bfloat16),
            grad_heads,
            preferred_element_type=jnp.float32,
        )
        key_part = jnp.einsum(
            "hqk,qhd->khd", grad_scores, query_heads, preferred_element_type=jnp.float32
        )
        grad_query = grad_query + jnp.einsum(
            "hqk,khd->qhd", grad_scores, key_block, preferred_element_type=jnp.float32
        )
        return (grad_query, (key_part, value_part))

    grad_query, (key_parts, value_parts) = lax.scan(
        back_pass,
        jnp.zeros((tok_rows, HEADS, head_width), jnp.float32),
        (key_stack, value_stack, block_shift),
    )
    grad_keys = key_parts[reach]
    grad_values = value_parts[reach]
    for position, distance in enumerate(distances):
        if distance != 0:
            got_pair = return_grads((key_parts[position], value_parts[position]), distance)
            grad_keys = grad_keys + got_pair[0]
            grad_values = grad_values + got_pair[1]
    query_low = grad_query.reshape(tok_rows, D).astype(jnp.bfloat16)
    key_low = grad_keys.reshape(tok_rows, D).astype(jnp.bfloat16)
    value_low = grad_values.reshape(tok_rows, D).astype(jnp.bfloat16)
    query_grad = rows_dot(normed, query_low)
    query_bias_grad = jnp.sum(query_low.astype(jnp.float32), axis=0)
    key_grad = rows_dot(normed, key_low)
    value_grad = rows_dot(normed, value_low)
    value_bias_grad = jnp.sum(value_low.astype(jnp.float32), axis=0)
    grad_normed = (
        back_dot(query_low, query_weight)
        + back_dot(key_low, key_weight)
        + back_dot(value_low, value_weight)
    )
    first_gain_grad = jnp.sum(grad_normed * first_hat, axis=0)
    first_bias_grad = jnp.sum(grad_normed, axis=0)
    input_grad = (grad_middle + norm_back(grad_normed, first_hat, first_dev, first_gain)).astype(
        jnp.bfloat16
    )
    packed = jnp.concatenate(
        [
            section.reshape(-1)
            for section in [
                first_gain_grad,
                first_bias_grad,
                query_grad,
                query_bias_grad,
                key_grad,
                value_grad,
                value_bias_grad,
                out_grad,
                out_bias_grad,
                second_gain_grad,
                second_bias_grad,
                up_grad,
                up_bias_grad,
                down_grad,
                down_bias_grad,
            ]
        ]
    )
    group_shard = lax.psum_scatter(
        packed.astype(jnp.bfloat16), "inner", scatter_dimension=0, tiled=True
    )
    grad_shard = lax.psum(group_shard, "outer").astype(jnp.float32)
    squares = lax.psum(jnp.sum(grad_shard * grad_shard), "inner")
    grad_norm = jnp.sqrt(squares)
    clipped = grad_shard / jnp.maximum(grad_norm, 1.0)
    moment_one = BETA_ONE * first_moment + (1.0 - BETA_ONE) * clipped
    moment_two = BETA_TWO * second_moment + (1.0 - BETA_TWO) * clipped * clipped
    shard_len = grad_shard.shape[0]
    own_weights = lax.dynamic_slice_in_dim(
        weights, lax.axis_index("inner") * shard_len, shard_len, 0
    ).astype(jnp.float32)
    update = moment_one / FIX_ONE / (jnp.sqrt(moment_two / FIX_TWO) + 1e-08) + DECAY * own_weights
    step_piece = update.astype(jnp.bfloat16)
    weight_step = lax.all_gather(step_piece, "inner", axis=0, tiled=True)
    return (layer_output, input_grad, grad_shard, grad_norm, moment_one, moment_two, weight_step)


def solution(mesh):
    return jax.shard_map(
        on_device,
        mesh=mesh,
        in_specs=(
            P(("outer", "inner"), None),
            P(),
            P(("outer", "inner"), None),
            P(),
            P("inner"),
            P("inner"),
        ),
        out_specs=(
            P(("outer", "inner"), None),
            P(("outer", "inner"), None),
            P("inner"),
            P(),
            P("inner"),
            P("inner"),
            P(),
        ),
        check_vma=False,
    )
```

profile of v0, /device:TPU:0, one launch (start us, length us, event | category | flops | bytes accessed | tf_op | source)
XLA Modules:
  0.0 1054.3 jit_solution(2918028599666637666)
XLA Ops:
  27.7 5.2 fusion.115
  49.2 7.0 collective-permute-done.7
  59.4 11.3 %collective-permute-start.1 = (bf16[512,512]{0,1:T(8,128)(2,1)}, bf16[512,512]{0,1:T(8,128)(2,1)}, u32[]{:S(2)}, u32[]{:S(2)}) collective-permute-start(bf16[512,512]{0,1:T(8,128)(2,1)} %fusion.69), channel_id=1, source_target_pairs={{0,2},{1,3},{2,4},{3,5},{4,6},{5,7},{6,8},{7,9},{8,10},{9,11},{10,... | collective-permute-start | bytes 1572872 | tf_op jit(solution)/shard_map/ppermute | solution.py:23
  81.6 87.1 %while.39 = (s32[]{:T(128)}, f32[8,512]{1,0:T(8,128)S(1)}, f32[8,512]{1,0:T(8,128)S(1)}, s32[7]{0:T(128)S(1)}, s32[]{:T(128)}, /*index=5*/s32[512]{0:T(512)S(1)}...) while((s32[]{:T(128)}, f32[8,512]{1,0:T(8,128)S(1)}, ...), condition=%wide.region_9.10_spmd.clone, body=%wide.region_6.9_spmd.clone.sunk | while | flops 283922944 | bytes 18833588 | solution.py:189
  83.1 5.8 fusion.179
  95.6 5.8 fusion.179
  108.0 5.8 fusion.179
  120.5 5.8 fusion.179
  132.9 5.8 fusion.179
  145.4 5.8 fusion.179
  157.8 5.8 fusion.179
  182.7 47.9 %while.40 = (s32[]{:T(128)}, f32[512,8,64]{0,2,1:T(8,128)}, bf16[7,512,8,64]{1,3,2,0:T(8,128)(2,1)}, s32[7]{0:T(128)S(1)}, s32[]{:T(128)}, /*index=5*/s32[512]{0...) while((s32[]{:T(128)}, f32[512,8,64]{0,2,1:T(8,128)}, ...), condition=%wide.region_11.12_spmd.clone, body=%wide.region_10.11_spmd.clone.sunk | while | flops 546570752 | bytes 4220598 | solution.py:208
  190.8 5.4 fusion.185
  197.7 5.4 fusion.185
  204.6 5.4 fusion.185
  211.5 5.4 fusion.185
  218.4 5.4 fusion.185
  225.3 5.4 fusion.185
  251.3 183.3 %while.41 = (s32[]{:T(128)}, f32[512,8,64]{0,2,1:T(8,128)S(1)}, f32[7,512,8,64]{1,3,2,0:T(8,128)}, f32[7,512,8,64]{1,3,2,0:T(8,128)}, bf16[7,512,8,64]{1,3,2,0:T...) while((s32[]{:T(128)}, f32[512,8,64]{0,2,1:T(8,128)S(1)}, ...), condition=%wide.region_18.19_spmd.clone, body=%wide.region_17.18_spmd.clone.sunk | while | flops 1366557184 | bytes 96788768 | solution.py:263
  251.5 5.6 fusion.196
  258.6 8.6 fusion.197
  277.6 5.6 fusion.196
  284.7 8.6 fusion.197
  303.8 5.6 fusion.196
  310.9 8.6 fusion.197
  330.0 5.6 fusion.196
  337.1 8.6 fusion.197
  356.1 5.6 fusion.196
  363.2 8.6 fusion.197
  382.3 5.6 fusion.196
  389.4 8.6 fusion.197
  408.4 5.6 fusion.196
  415.5 8.6 fusion.197
  440.0 20.0 %collective-permute-start.23 = (bf16[512,8,64]{0,2,1:T(8,128)(2,1)}, bf16[512,8,64]{0,2,1:T(8,128)(2,1)}, u32[]{:S(2)}, u32[]{:S(2)}) collective-permute-start(bf16[512,8,64]{0,2,1:T(8,128)(2,1)} %get-tuple-element.446), channel_id=1, source_target_pairs={{0,3},{1,4},{2,5},{3,6},{4,7},{5,8},{6,9},{7,10},{8,11},{9,12},{10... | collective-permute-start | bytes 1572872 | tf_op jit(solution)/shard_map/ppermute | solution.py:23
  460.0 9.7 collective-permute-start.22
  481.6 22.4 %collective-permute-done.22 = bf16[512,8,64]{0,2,1:T(8,128)(2,1)} collective-permute-done((bf16[512,8,64]{0,2,1:T(8,128)(2,1)}, bf16[512,8,64]{0,2,1:T(8,128)(2,1)}, u32[]{:S(2)}, u32[]{:S(2)}) %collective-permute-start.22) | collective-permute-done | bytes 524320 | tf_op jit(solution)/shard_map/ppermute | solution.py:23
  529.3 18.1 %collective-permute-done.13 = bf16[512,8,64]{0,2,1:T(8,128)(2,1)S(1)} collective-permute-done((bf16[512,8,64]{0,2,1:T(8,128)(2,1)S(1)}, bf16[512,8,64]{0,2,1:T(8,128)(2,1)S(1)}, u32[]{:S(2)}, u32[]{:S(2)}) %collective-permute-start.13) | collective-permute-done | bytes 524320 | tf_op jit(solution)/shard_map/ppermute | solution.py:23
  564.2 9.1 dynamic-update-slice.4
  573.2 9.1 dynamic-update-slice.5
  588.8 33.0 %dynamic-update-slice.11 = bf16[3151872]{0:T(1024)(128)(2,1)} dynamic-update-slice(bf16[3151872]{0:T(1024)(128)(2,1)} %dynamic-update-slice.10, bf16[1048576]{0:T(1024)(128)(2,1)} %bitcast.268, s32[]{} %constant.145) | dynamic-update-slice | bytes 4194308
  623.3 32.9 %dynamic-update-slice.13 = bf16[3151872]{0:T(1024)(128)(2,1)} dynamic-update-slice(bf16[3151872]{0:T(1024)(128)(2,1)} %dynamic-update-slice.12, bf16[1048576]{0:T(1024)(128)(2,1)} %bitcast.267, s32[]{} %constant.147) | dynamic-update-slice | bytes 4194308
  658.9 139.7 %all-reduce.6.cloned.1.call-done = bf16[3151872]{0:T(1024)(128)(2,1)} async-done(((bf16[3151872]{0:T(1024)(128)(2,1)}), bf16[3151872]{0:T(1024)(128)(2,1)}) %all-reduce.6.cloned.1.call-update) | async-done | bytes 6303760
  802.1 91.0 %all-reduce.4.cloned.1.call-done = bf16[787968]{0:T(1024)(128)(2,1)} async-done(((bf16[787968]{0:T(1024)(128)(2,1)}), bf16[787968]{0:T(1024)(128)(2,1)}) %all-reduce.4.cloned.1.call-update) | async-done | bytes 1575952 | tf_op jit(solution)/shard_map/psum | solution.py:318
  897.5 7.6 psum.15
  905.8 7.4 add_convert_fusion
  923.8 73.4 %all-gather.3.cloned.1.call-done = bf16[4,1,787968]{2,1,0:T(2,128)(2,1)} async-done(((bf16[1,1,787968]{2,1,0:T(2,128)(2,1)}), bf16[4,1,787968]{2,1,0:T(2,128)(2,1)}) %all-gather.3.cloned.1.call-update) | async-done | bytes 6303760 | tf_op jit(solution)/shard_map/all_gather | solution.py:330
  997.1 41.4 %reduce.7 = bf16[4,787968]{1,0:T(4,128)(2,1)} reduce(bf16[4,1,787968]{2,1,0:T(2,128)(2,1)} %all-gather.3.cloned.1.call-done, bf16[]{:T(256)} %constant.133), dimensions={1}, to_apply=%all-gather.reduce_sub_computation | reduce | bytes 12607490 | tf_op jit(solution)/shard_map/all_gather | solution.py:330
  1038.5 7.9 reshape.423
  (372 shorter events, 304.3 us)
Async XLA Ops:
  7.2 791.4 %all-reduce.6.cloned.1.call-start = ((), (), s32[]{:S(2)}) async-start(), calls=%async_computation.2 | async-start | bytes 12607488
  8.7 26.5 %copy-start.28 = (f32[512]{0:T(512)}, f32[512]{0:T(512)S(1)}, u32[]{:S(2)}) copy-start(f32[512]{0:T(512)S(1)} %get-tuple-element.438) | copy-start | bytes 6148
  8.7 26.5 %copy-start.33 = (f32[512]{0:T(512)}, f32[512]{0:T(512)S(1)}, u32[]{:S(2)}) copy-start(f32[512]{0:T(512)S(1)} %get-tuple-element.437) | copy-start | bytes 6148
  10.8 24.4 %copy-start.26 = (f32[512]{0:T(512)}, f32[512]{0:T(512)S(1)}, u32[]{:S(2)}) copy-start(f32[512]{0:T(512)S(1)} %broadcast_multiply_fusion.5) | copy-start | bytes 6148
  11.0 24.2 %copy-start.30 = (f32[512]{0:T(512)}, f32[512]{0:T(512)S(1)}, u32[]{:S(2)}) copy-start(f32[512]{0:T(512)S(1)} %add_rsqrt_fusion.1) | copy-start | bytes 6148
  11.3 21.6 %copy-start.16 = (bf16[512,512]{1,0:T(8,128)(2,1)}, bf16[512,512]{1,0:T(8,128)(2,1)S(1)}, u32[]{:S(2)}) copy-start(bf16[512,512]{1,0:T(8,128)(2,1)S(1)} %slice.155) | copy-start | bytes 1572868
  12.8 34.1 %collective-permute-start.6 = (bf16[512,512]{0,1:T(8,128)(2,1)}, bf16[512,512]{0,1:T(8,128)(2,1)}, u32[]{:S(2)}, u32[]{:S(2)}) collective-permute-start(bf16[512,512]{0,1:T(8,128)(2,1)} %convolution_convert_fusion.7), channel_id=1, source_target_pairs={{0,3},{1,4},{2,5},{3,6},{4,7},{5,8},{6,9},{7,10},{8,11},{9,12},{10... | collective-permute-start | bytes 1572872 | tf_op jit(solution)/shard_map/ppermute | solution.py:23
  17.9 38.3 %collective-permute-start.7 = (bf16[512,512]{0,1:T(8,128)(2,1)}, bf16[512,512]{0,1:T(8,128)(2,1)}, u32[]{:S(2)}, u32[]{:S(2)}) collective-permute-start(bf16[512,512]{0,1:T(8,128)(2,1)} %convolution_convert_fusion.7), channel_id=1, source_target_pairs={{0,2},{1,3},{2,4},{3,5},{4,6},{5,7},{6,8},{7,9},{8,10},{9,11},{10,... | collective-permute-start | bytes 1572872 | tf_op jit(solution)/shard_map/ppermute | solution.py:23
  22.1 37.3 %collective-permute-start.8 = (bf16[512,512]{0,1:T(8,128)(2,1)}, bf16[512,512]{0,1:T(8,128)(2,1)}, u32[]{:S(2)}, u32[]{:S(2)}) collective-permute-start(bf16[512,512]{0,1:T(8,128)(2,1)} %convolution_convert_fusion.7), channel_id=1, source_target_pairs={{0,1},{1,2},{2,3},{3,4},{4,5},{5,6},{6,7},{7,8},{8,9},{9,10},{10,1... | collective-permute-start | bytes 1572872 | tf_op jit(solution)/shard_map/ppermute | solution.py:23
  24.4 48.4 %collective-permute-start.9 = (bf16[512,512]{0,1:T(8,128)(2,1)}, bf16[512,512]{0,1:T(8,128)(2,1)}, u32[]{:S(2)}, u32[]{:S(2)}) collective-permute-start(bf16[512,512]{0,1:T(8,128)(2,1)} %convolution_convert_fusion.7), channel_id=1, source_target_pairs={{1,0},{2,1},{3,2},{4,3},{5,4},{6,5},{7,6},{8,7},{9,8},{10,9},{11,1... | collective-permute-start | bytes 1572872 | tf_op jit(solution)/shard_map/ppermute | solution.py:23
  25.7 50.3 %collective-permute-start.10 = (bf16[512,512]{0,1:T(8,128)(2,1)}, bf16[512,512]{0,1:T(8,128)(2,1)}, u32[]{:S(2)}, u32[]{:S(2)}) collective-permute-start(bf16[512,512]{0,1:T(8,128)(2,1)} %convolution_convert_fusion.7), channel_id=1, source_target_pairs={{2,0},{3,1},{4,2},{5,3},{6,4},{7,5},{8,6},{9,7},{10,8},{11,9},{12,... | collective-permute-start | bytes 1572872 | tf_op jit(solution)/shard_map/ppermute | solution.py:23
  37.2 8.6 copy-start.12
  46.8 31.6 %collective-permute-start.11 = (bf16[512,512]{0,1:T(8,128)(2,1)}, bf16[512,512]{0,1:T(8,128)(2,1)S(1)}, u32[]{:S(2)}, u32[]{:S(2)}) collective-permute-start(bf16[512,512]{0,1:T(8,128)(2,1)} %convolution_convert_fusion.7), channel_id=1, source_target_pairs={{3,0},{4,1},{5,2},{6,3},{7,4},{8,5},{9,6},{10,7},{11,8},{12,9},{13... | collective-permute-start | bytes 1572872 | tf_op jit(solution)/shard_map/ppermute | solution.py:23
  56.2 112.5 %collective-permute-start = (bf16[512,512]{0,1:T(8,128)(2,1)}, bf16[512,512]{0,1:T(8,128)(2,1)}, u32[]{:S(2)}, u32[]{:S(2)}) collective-permute-start(bf16[512,512]{0,1:T(8,128)(2,1)} %fusion.69), channel_id=1, source_target_pairs={{0,3},{1,4},{2,5},{3,6},{4,7},{5,8},{6,9},{7,10},{8,11},{9,12},{10... | collective-permute-start | bytes 1572872 | tf_op jit(solution)/shard_map/ppermute | solution.py:23
  59.4 111.9 %collective-permute-start.1 = (bf16[512,512]{0,1:T(8,128)(2,1)}, bf16[512,512]{0,1:T(8,128)(2,1)}, u32[]{:S(2)}, u32[]{:S(2)}) collective-permute-start(bf16[512,512]{0,1:T(8,128)(2,1)} %fusion.69), channel_id=1, source_target_pairs={{0,2},{1,3},{2,4},{3,5},{4,6},{5,7},{6,8},{7,9},{8,10},{9,11},{10,... | collective-permute-start | bytes 1572872 | tf_op jit(solution)/shard_map/ppermute | solution.py:23
  72.8 99.6 %collective-permute-start.2 = (bf16[512,512]{0,1:T(8,128)(2,1)}, bf16[512,512]{0,1:T(8,128)(2,1)}, u32[]{:S(2)}, u32[]{:S(2)}) collective-permute-start(bf16[512,512]{0,1:T(8,128)(2,1)} %fusion.69), channel_id=1, source_target_pairs={{0,1},{1,2},{2,3},{3,4},{4,5},{5,6},{6,7},{7,8},{8,9},{9,10},{10,1... | collective-permute-start | bytes 1572872 | tf_op jit(solution)/shard_map/ppermute | solution.py:23
  76.0 98.5 %collective-permute-start.3 = (bf16[512,512]{0,1:T(8,128)(2,1)}, bf16[512,512]{0,1:T(8,128)(2,1)}, u32[]{:S(2)}, u32[]{:S(2)}) collective-permute-start(bf16[512,512]{0,1:T(8,128)(2,1)} %fusion.69), channel_id=1, source_target_pairs={{1,0},{2,1},{3,2},{4,3},{5,4},{6,5},{7,6},{8,7},{9,8},{10,9},{11,1... | collective-permute-start | bytes 1572872 | tf_op jit(solution)/shard_map/ppermute | solution.py:23
  78.4 97.2 %collective-permute-start.4 = (bf16[512,512]{0,1:T(8,128)(2,1)}, bf16[512,512]{0,1:T(8,128)(2,1)}, u32[]{:S(2)}, u32[]{:S(2)}) collective-permute-start(bf16[512,512]{0,1:T(8,128)(2,1)} %fusion.69), channel_id=1, source_target_pairs={{2,0},{3,1},{4,2},{5,3},{6,4},{7,5},{8,6},{9,7},{10,8},{11,9},{12,... | collective-permute-start | bytes 1572872 | tf_op jit(solution)/shard_map/ppermute | solution.py:23
  168.7 12.1 %collective-permute-start.5 = (bf16[512,512]{0,1:T(8,128)(2,1)}, bf16[512,512]{0,1:T(8,128)(2,1)S(1)}, u32[]{:S(2)}, u32[]{:S(2)}) collective-permute-start(bf16[512,512]{0,1:T(8,128)(2,1)} %fusion.69), channel_id=1, source_target_pairs={{3,0},{4,1},{5,2},{6,3},{7,4},{8,5},{9,6},{10,7},{11,8},{12,9},{13... | collective-permute-start | bytes 1572872 | tf_op jit(solution)/shard_map/ppermute | solution.py:23
  267.2 6.2 copy-start.1
  293.4 6.2 copy-start.1
  319.5 6.2 copy-start.1
  345.7 6.2 copy-start.1
  371.9 6.2 copy-start.1
  398.0 6.2 copy-start.1
  424.2 6.2 copy-start.1
  438.2 31.4 %copy-start.14 = (bf16[512,512]{1,0:T(8,128)(2,1)S(1)}, bf16[512,512]{1,0:T(8,128)(2,1)}, u32[]{:S(2)}) copy-start(bf16[512,512]{1,0:T(8,128)(2,1)} %param.14) | copy-start | bytes 1572868
  440.0 40.3 %collective-permute-start.23 = (bf16[512,8,64]{0,2,1:T(8,128)(2,1)}, bf16[512,8,64]{0,2,1:T(8,128)(2,1)}, u32[]{:S(2)}, u32[]{:S(2)}) collective-permute-start(bf16[512,8,64]{0,2,1:T(8,128)(2,1)} %get-tuple-element.446), channel_id=1, source_target_pairs={{0,3},{1,4},{2,5},{3,6},{4,7},{5,8},{6,9},{7,10},{8,11},{9,12},{10... | collective-permute-start | bytes 1572872 | tf_op jit(solution)/shard_map/ppermute | solution.py:23
  460.0 44.0 %collective-permute-start.22 = (bf16[512,8,64]{0,2,1:T(8,128)(2,1)}, bf16[512,8,64]{0,2,1:T(8,128)(2,1)}, u32[]{:S(2)}, u32[]{:S(2)}) collective-permute-start(bf16[512,8,64]{0,2,1:T(8,128)(2,1)} %get-tuple-element.447), channel_id=1, source_target_pairs={{0,2},{1,3},{2,4},{3,5},{4,6},{5,7},{6,8},{7,9},{8,10},{9,11},{10,... | collective-permute-start | bytes 1572872 | tf_op jit(solution)/shard_map/ppermute | solution.py:23
  469.8 45.2 %collective-permute-start.21 = (bf16[512,8,64]{0,2,1:T(8,128)(2,1)}, bf16[512,8,64]{0,2,1:T(8,128)(2,1)S(1)}, u32[]{:S(2)}, u32[]{:S(2)}) collective-permute-start(bf16[512,8,64]{0,2,1:T(8,128)(2,1)} %get-tuple-element.448), channel_id=1, source_target_pairs={{0,1},{1,2},{2,3},{3,4},{4,5},{5,6},{6,7},{7,8},{8,9},{9,10},{10,1... | collective-permute-start | bytes 1572872 | tf_op jit(solution)/shard_map/ppermute | solution.py:23
  472.1 45.1 %collective-permute-start.20 = (bf16[512,8,64]{0,2,1:T(8,128)(2,1)}, bf16[512,8,64]{0,2,1:T(8,128)(2,1)S(1)}, u32[]{:S(2)}, u32[]{:S(2)}) collective-permute-start(bf16[512,8,64]{0,2,1:T(8,128)(2,1)} %get-tuple-element.449), channel_id=1, source_target_pairs={{1,0},{2,1},{3,2},{4,3},{5,4},{6,5},{7,6},{8,7},{9,8},{10,9},{11,1... | collective-permute-start | bytes 1572872 | tf_op jit(solution)/shard_map/ppermute | solution.py:23
  473.4 46.5 %collective-permute-start.19 = (bf16[512,8,64]{0,2,1:T(8,128)(2,1)}, bf16[512,8,64]{0,2,1:T(8,128)(2,1)S(1)}, u32[]{:S(2)}, u32[]{:S(2)}) collective-permute-start(bf16[512,8,64]{0,2,1:T(8,128)(2,1)} %get-tuple-element.450), channel_id=1, source_target_pairs={{2,0},{3,1},{4,2},{5,3},{6,4},{7,5},{8,6},{9,7},{10,8},{11,9},{12,... | collective-permute-start | bytes 1572872 | tf_op jit(solution)/shard_map/ppermute | solution.py:23
  479.0 28.9 %copy-start.39 = (bf16[512,2048]{1,0:T(8,128)(2,1)S(1)}, bf16[512,2048]{1,0:T(8,128)(2,1)}, u32[]{:S(2)}) copy-start(bf16[512,2048]{1,0:T(8,128)(2,1)} %copy-done.38) | copy-start | bytes 6291460
  480.3 40.9 %collective-permute-start.18 = (bf16[512,8,64]{0,2,1:T(8,128)(2,1)S(1)}, bf16[512,8,64]{0,2,1:T(8,128)(2,1)S(1)}, u32[]{:S(2)}, u32[]{:S(2)}) collective-permute-start(bf16[512,8,64]{0,2,1:T(8,128)(2,1)S(1)} %copy-done.20), channel_id=1, source_target_pairs={{3,0},{4,1},{5,2},{6,3},{7,4},{8,5},{9,6},{10,7},{11,8},{12,9},{13... | collective-permute-start | bytes 1572872 | tf_op jit(solution)/shard_map/ppermute | solution.py:23
  504.0 18.6 %collective-permute-start.17 = (bf16[512,8,64]{0,2,1:T(8,128)(2,1)S(1)}, bf16[512,8,64]{0,2,1:T(8,128)(2,1)S(1)}, u32[]{:S(2)}, u32[]{:S(2)}) collective-permute-start(bf16[512,8,64]{0,2,1:T(8,128)(2,1)S(1)} %get-tuple-element.452), channel_id=1, source_target_pairs={{0,3},{1,4},{2,5},{3,6},{4,7},{5,8},{6,9},{7,10},{8,11},{9,12},{10... | collective-permute-start | bytes 1572872 | tf_op jit(solution)/shard_map/ppermute | solution.py:23
  514.9 11.1 %copy-start.27 = (f32[512]{0:T(512)S(1)}, f32[512]{0:T(512)}, u32[]{:S(2)}) copy-start(f32[512]{0:T(512)} %copy-done.26) | copy-start | bytes 6148
  514.9 11.1 %copy-start.29 = (f32[512]{0:T(512)S(1)}, f32[512]{0:T(512)}, u32[]{:S(2)}) copy-start(f32[512]{0:T(512)} %copy-done.28) | copy-start | bytes 6148
  515.0 11.1 %copy-start.31 = (f32[512]{0:T(512)S(1)}, f32[512]{0:T(512)}, u32[]{:S(2)}) copy-start(f32[512]{0:T(512)} %copy-done.30) | copy-start | bytes 6148
  515.0 11.1 %copy-start.34 = (f32[512]{0:T(512)S(1)}, f32[512]{0:T(512)}, u32[]{:S(2)}) copy-start(f32[512]{0:T(512)} %copy-done.33) | copy-start | bytes 6148
  515.0 14.4 %collective-permute-start.16 = (bf16[512,8,64]{0,2,1:T(8,128)(2,1)S(1)}, bf16[512,8,64]{0,2,1:T(8,128)(2,1)S(1)}, u32[]{:S(2)}, u32[]{:S(2)}) collective-permute-start(bf16[512,8,64]{0,2,1:T(8,128)(2,1)S(1)} %get-tuple-element.453), channel_id=1, source_target_pairs={{0,2},{1,3},{2,4},{3,5},{4,6},{5,7},{6,8},{7,9},{8,10},{9,11},{10,... | collective-permute-start | bytes 1572872 | tf_op jit(solution)/shard_map/ppermute | solution.py:23
  517.2 12.2 %collective-permute-start.15 = (bf16[512,8,64]{0,2,1:T(8,128)(2,1)S(1)}, bf16[512,8,64]{0,2,1:T(8,128)(2,1)S(1)}, u32[]{:S(2)}, u32[]{:S(2)}) collective-permute-start(bf16[512,8,64]{0,2,1:T(8,128)(2,1)S(1)} %get-tuple-element.454), channel_id=1, source_target_pairs={{0,1},{1,2},{2,3},{3,4},{4,5},{5,6},{6,7},{7,8},{8,9},{9,10},{10,1... | collective-permute-start | bytes 1572872 | tf_op jit(solution)/shard_map/ppermute | solution.py:23
  519.9 9.4 collective-permute-start.14
  521.2 26.3 %collective-permute-start.13 = (bf16[512,8,64]{0,2,1:T(8,128)(2,1)S(1)}, bf16[512,8,64]{0,2,1:T(8,128)(2,1)S(1)}, u32[]{:S(2)}, u32[]{:S(2)}) collective-permute-start(bf16[512,8,64]{0,2,1:T(8,128)(2,1)S(1)} %get-tuple-element.456), channel_id=1, source_target_pairs={{2,0},{3,1},{4,2},{5,3},{6,4},{7,5},{8,6},{9,7},{10,8},{11,9},{12,... | collective-permute-start | bytes 1572872 | tf_op jit(solution)/shard_map/ppermute | solution.py:23
  522.5 26.3 %collective-permute-start.12 = (bf16[512,8,64]{0,2,1:T(8,128)(2,1)S(1)}, bf16[512,8,64]{0,2,1:T(8,128)(2,1)S(1)}, u32[]{:S(2)}, u32[]{:S(2)}) collective-permute-start(bf16[512,8,64]{0,2,1:T(8,128)(2,1)S(1)} %get-tuple-element.451), channel_id=1, source_target_pairs={{3,0},{4,1},{5,2},{6,3},{7,4},{8,5},{9,6},{10,7},{11,8},{12,9},{13... | collective-permute-start | bytes 1572872 | tf_op jit(solution)/shard_map/ppermute | solution.py:23
  527.0 24.9 %copy-start.17 = (bf16[512,512]{1,0:T(8,128)(2,1)S(1)}, bf16[512,512]{1,0:T(8,128)(2,1)}, u32[]{:S(2)}) copy-start(bf16[512,512]{1,0:T(8,128)(2,1)} %copy-done.16) | copy-start | bytes 1572868
  555.4 28.3 %copy-start.15 = (bf16[64,4,8,128]{3,1,2,0:T(4,128)(2,1)S(1)}, bf16[64,4,8,128]{3,1,2,0:T(4,128)(2,1)}, u32[]{:S(2)}) copy-start(bf16[64,4,8,128]{3,1,2,0:T(4,128)(2,1)} %copy.86) | copy-start | bytes 1572868
  657.6 235.4 %all-reduce.4.cloned.1.call-start = ((), (), s32[]{:S(2)}) async-start(), calls=%async_computation | async-start | bytes 3153920 | tf_op jit(solution)/shard_map/psum | solution.py:318
  802.0 195.1 %all-gather.3.cloned.1.call-start = ((), (), s32[]{:S(2)}) async-start(), calls=%async_computation.1 | async-start | bytes 15759360 | tf_op jit(solution)/shard_map/all_gather | solution.py:330
  (31 other events, 96.8 us)
Sparse Core Ops, SparseCore 0:
  657.8 140.7 all-reduce.5
  802.8 90.2 all-reduce.3
  916.5 80.5 all-gather.2
where the time goes:
time: 1080 us; the launch traced here: 1050 us
  waiting for transfers between devices  359 us (33%)
  matrix products  273 us (25%)
  local copies, waits for them, and re-layouts  182 us (17%)
  other arithmetic  116 us (11%)
  starting transfers between devices  83.7 us (8%)
  between operations  17.4 us (2%)
  loops' own time  14.6 us (1%)
    unnamed x116, local copies, waits for them, and re-layouts  143 us
    unnamed x4, waiting for transfers between devices  140 us
    psum x1, waiting for transfers between devices, on_device(): grad_shard = lax.psum(group_shard, 'outer').astype(jnp.float32)  91 us
    ppermute x24, starting transfers between devices, passed_along(): return lax.ppermute(block, axis, route)  83.6 us
    dot_general x14, matrix products, block_scores(): jnp.einsum('qhd,khd->hqk', query_heads, key_block, preferred_element_type...  79.3 us
    all_gather x1, waiting for transfers between devices, on_device(): weight_step = lax.all_gather(step_piece, 'inner', axis=0, tiled=True)  73.4 us
    dot_general x7, matrix products, back_pass(): jnp.einsum('qhd,khd->hqk', grad_heads, value_block, preferred_element_typ...  60.5 us
    ppermute x24, waiting for transfers between devices, passed_along(): return lax.ppermute(block, axis, route)  55.3 us
  transfers between devices with their start and end apart: 27, of which 9 were waited for; matrix products, arithmetic and copies ran while one was open for 13% of the time, Pallas kernels for 0%

commit v1 on v0

--- a/solution.py
+++ b/solution.py
@@ -315,7 +315,7 @@
     group_shard = lax.psum_scatter(
         packed.astype(jnp.bfloat16), "inner", scatter_dimension=0, tiled=True
     )
-    grad_shard = lax.psum(group_shard, "outer").astype(jnp.float32)
+    grad_shard = jnp.sum(lax.all_gather(group_shard, "outer"), axis=0).astype(jnp.float32)
     squares = lax.psum(jnp.sum(grad_shard * grad_shard), "inner")
     grad_norm = jnp.sqrt(squares)
     clipped = grad_shard / jnp.maximum(grad_norm, 1.0)

time: 1080 us -> 1600 us (1.48)
  waiting for transfers between devices: 359 us -> 751 us
  other arithmetic: 116 us -> 248 us
    all_gather x0 -> x1, waiting for transfers between devices: none -> 481 us  [on_device(): lax.all_gather(group_shard, 'outer')]
    reduce_sum x0 -> x1, other arithmetic: none -> 132 us  [on_device(): jnp.sum(lax.all_gather(group_shard, 'outer'), axis=0).astype(jnp.float32)]
    psum x1 -> x0, waiting for transfers between devices: 91 us -> none  [on_device(): grad_shard = lax.psum(group_shard, 'outer').astype(jnp.float32)]
    unnamed x116 -> x121, local copies, waits for them, and re-layouts: 143 us -> 144 us
  transfers between devices with their start and end apart: 27 -> 27, of which waited for: 9 -> 9; matrix products, arithmetic and copies ran while one was open for 13% -> 9% of each run, Pallas kernels for 0% -> 0%
where the time goes in v1:
time: 1600 us; the launch traced here: 1580 us
  waiting for transfers between devices  751 us (47%)
  matrix products  273 us (17%)
  other arithmetic  248 us (16%)
  local copies, waits for them, and re-layouts  184 us (12%)
  starting transfers between devices  83.9 us (5%)
  between operations  17.6 us (1%)
    all_gather x1, waiting for transfers between devices, on_device(): lax.all_gather(group_shard, 'outer')  481 us
    unnamed x121, local copies, waits for them, and re-layouts  144 us
    unnamed x4, waiting for transfers between devices  140 us
    reduce_sum x1, other arithmetic, on_device(): jnp.sum(lax.all_gather(group_shard, 'outer'), axis=0).astype(jnp.float32)  132 us
    ppermute x24, starting transfers between devices, passed_along(): return lax.ppermute(block, axis, route)  83.5 us
    dot_general x14, matrix products, block_scores(): jnp.einsum('qhd,khd->hqk', query_heads, key_block, preferred_element_type...  79.2 us
    all_gather x1, waiting for transfers between devices, on_device(): weight_step = lax.all_gather(step_piece, 'inner', axis=0, tiled=True)  74.5 us
    dot_general x7, matrix products, back_pass(): jnp.einsum('qhd,khd->hqk', grad_heads, value_block, preferred_element_typ...  60.5 us
  transfers between devices with their start and end apart: 27, of which 9 were waited for; matrix products, arithmetic and copies ran while one was open for 9% of the time, Pallas kernels for 0%

profile of v1, /device:TPU:0, one launch (start us, length us, event | category | flops | bytes accessed | tf_op | source)
XLA Modules:
  0.0 1579.5 jit_solution(12020607646645677668)
XLA Ops:
  49.3 6.8 collective-permute-done.7
  59.3 11.5 collective-permute-start.1
  81.7 87.0 %while.39 = (s32[]{:T(128)}, f32[8,512]{1,0:T(8,128)S(1)}, f32[8,512]{1,0:T(8,128)S(1)}, s32[7]{0:T(128)S(1)}, s32[]{:T(128)}, /*index=5*/s32[512]{0:T(512)S(1)}...) while((s32[]{:T(128)}, f32[8,512]{1,0:T(8,128)S(1)}, ...), condition=%wide.region_9.10_spmd.clone, body=%wide.region_6.9_spmd.clone.sunk | while | flops 283922944 | bytes 18833588 | solution.py:189
  83.2 5.7 fusion.179
  95.7 5.7 fusion.179
  108.1 5.7 fusion.179
  120.5 5.7 fusion.179
  133.0 5.7 fusion.179
  145.4 5.7 fusion.179
  157.8 5.7 fusion.179
  182.6 47.9 %while.40 = (s32[]{:T(128)}, f32[512,8,64]{0,2,1:T(8,128)}, bf16[7,512,8,64]{1,3,2,0:T(8,128)(2,1)}, s32[7]{0:T(128)S(1)}, s32[]{:T(128)}, /*index=5*/s32[512]{0...) while((s32[]{:T(128)}, f32[512,8,64]{0,2,1:T(8,128)}, ...), condition=%wide.region_11.12_spmd.clone, body=%wide.region_10.11_spmd.clone.sunk | while | flops 546570752 | bytes 4220598 | solution.py:208
  190.7 5.4 fusion.185
  197.6 5.4 fusion.185
  204.4 5.4 fusion.185
  211.3 5.4 fusion.185
  218.2 5.4 fusion.185
  225.1 5.4 fusion.185
  251.1 183.4 %while.41 = (s32[]{:T(128)}, f32[512,8,64]{0,2,1:T(8,128)S(1)}, f32[7,512,8,64]{1,3,2,0:T(8,128)}, f32[7,512,8,64]{1,3,2,0:T(8,128)}, bf16[7,512,8,64]{1,3,2,0:T...) while((s32[]{:T(128)}, f32[512,8,64]{0,2,1:T(8,128)S(1)}, ...), condition=%wide.region_18.19_spmd.clone, body=%wide.region_17.18_spmd.clone.sunk | while | flops 1366557184 | bytes 96788768 | solution.py:263
  251.5 5.6 fusion.196
  258.6 8.6 fusion.197
  277.6 5.6 fusion.196
  284.7 8.6 fusion.197
  303.8 5.6 fusion.196
  310.9 8.6 fusion.197
  329.9 5.6 fusion.196
  337.0 8.6 fusion.197
  356.1 5.6 fusion.196
  363.2 8.6 fusion.197
  382.2 5.6 fusion.196
  389.3 8.6 fusion.197
  408.3 5.6 fusion.196
  415.4 8.6 fusion.197
  439.9 19.9 %collective-permute-start.23 = (bf16[512,8,64]{0,2,1:T(8,128)(2,1)}, bf16[512,8,64]{0,2,1:T(8,128)(2,1)}, u32[]{:S(2)}, u32[]{:S(2)}) collective-permute-start(bf16[512,8,64]{0,2,1:T(8,128)(2,1)} %get-tuple-element.446), channel_id=1, source_target_pairs={{0,3},{1,4},{2,5},{3,6},{4,7},{5,8},{6,9},{7,10},{8,11},{9,12},{10... | collective-permute-start | bytes 1572872 | tf_op jit(solution)/shard_map/ppermute | solution.py:23
  459.8 9.7 collective-permute-start.22
  481.4 22.4 %collective-permute-done.22 = bf16[512,8,64]{0,2,1:T(8,128)(2,1)} collective-permute-done((bf16[512,8,64]{0,2,1:T(8,128)(2,1)}, bf16[512,8,64]{0,2,1:T(8,128)(2,1)}, u32[]{:S(2)}, u32[]{:S(2)}) %collective-permute-start.22) | collective-permute-done | bytes 524320 | tf_op jit(solution)/shard_map/ppermute | solution.py:23
  529.0 18.2 %collective-permute-done.13 = bf16[512,8,64]{0,2,1:T(8,128)(2,1)S(1)} collective-permute-done((bf16[512,8,64]{0,2,1:T(8,128)(2,1)S(1)}, bf16[512,8,64]{0,2,1:T(8,128)(2,1)S(1)}, u32[]{:S(2)}, u32[]{:S(2)}) %collective-permute-start.13) | collective-permute-done | bytes 524320 | tf_op jit(solution)/shard_map/ppermute | solution.py:23
  563.9 9.1 dynamic-update-slice.4
  572.9 9.1 dynamic-update-slice.5
  588.5 33.0 %dynamic-update-slice.11 = bf16[3151872]{0:T(1024)(128)(2,1)} dynamic-update-slice(bf16[3151872]{0:T(1024)(128)(2,1)} %dynamic-update-slice.10, bf16[1048576]{0:T(1024)(128)(2,1)} %bitcast.268, s32[]{} %constant.147) | dynamic-update-slice | bytes 4194308
  623.0 32.9 %dynamic-update-slice.13 = bf16[3151872]{0:T(1024)(128)(2,1)} dynamic-update-slice(bf16[3151872]{0:T(1024)(128)(2,1)} %dynamic-update-slice.12, bf16[1048576]{0:T(1024)(128)(2,1)} %bitcast.267, s32[]{} %constant.149) | dynamic-update-slice | bytes 4194308
  658.6 139.8 %all-reduce.3.cloned.1.call-done = bf16[3151872]{0:T(1024)(128)(2,1)} async-done(((bf16[3151872]{0:T(1024)(128)(2,1)}), bf16[3151872]{0:T(1024)(128)(2,1)}) %all-reduce.3.cloned.1.call-update) | async-done | bytes 6303760
  804.1 481.3 %all-gather.6.cloned.1.call-done = bf16[8,1,787968]{2,1,0:T(2,128)(2,1)} async-done(((bf16[1,1,787968]{2,1,0:T(2,128)(2,1)}), bf16[8,1,787968]{2,1,0:T(2,128)(2,1)}) %all-gather.6.cloned.1.call-update) | async-done | bytes 12607504 | tf_op jit(solution)/shard_map/all_gather | solution.py:318
  1285.4 132.1 %reduce_sum.246 = bf16[787968]{0:T(1024)(128)(2,1)} reduce(bf16[8,1,787968]{2,1,0:T(2,128)(2,1)} %all-gather.6.cloned.1.call-done, bf16[]{:T(256)} %constant.116.clone.1), dimensions={0,1}, to_apply=%region_31.32 | reduce | flops 5515776 | bytes 14183426 | tf_op jit(solution)/shard_map/reduce_sum | solution.py:318
  1421.9 7.0 psum.7
  1429.6 7.4 add_convert_fusion
  1447.6 74.5 %all-gather.8.cloned.1.call-done = bf16[4,1,787968]{2,1,0:T(2,128)(2,1)} async-done(((bf16[1,1,787968]{2,1,0:T(2,128)(2,1)}), bf16[4,1,787968]{2,1,0:T(2,128)(2,1)}) %all-gather.8.cloned.1.call-update) | async-done | bytes 6303760 | tf_op jit(solution)/shard_map/all_gather | solution.py:330
  1522.1 41.4 %reduce.9 = bf16[4,787968]{1,0:T(4,128)(2,1)} reduce(bf16[4,1,787968]{2,1,0:T(2,128)(2,1)} %all-gather.8.cloned.1.call-done, bf16[]{:T(256)} %constant.135), dimensions={1}, to_apply=%all-gather.2.reduce_sub_computation | reduce | bytes 12607490 | tf_op jit(solution)/shard_map/all_gather | solution.py:330
  1563.5 7.9 reshape.426
  (378 shorter events, 311.4 us)
Async XLA Ops:
  7.2 791.2 %all-reduce.3.cloned.1.call-start = ((), (), s32[]{:S(2)}) async-start(), calls=%async_computation.2 | async-start | bytes 12607488
  8.7 26.6 %copy-start.30 = (f32[512]{0:T(512)}, f32[512]{0:T(512)S(1)}, u32[]{:S(2)}) copy-start(f32[512]{0:T(512)S(1)} %get-tuple-element.438) | copy-start | bytes 6148
  8.7 26.6 %copy-start.35 = (f32[512]{0:T(512)}, f32[512]{0:T(512)S(1)}, u32[]{:S(2)}) copy-start(f32[512]{0:T(512)S(1)} %get-tuple-element.437) | copy-start | bytes 6148
  10.8 24.4 %copy-start.28 = (f32[512]{0:T(512)}, f32[512]{0:T(512)S(1)}, u32[]{:S(2)}) copy-start(f32[512]{0:T(512)S(1)} %broadcast_multiply_fusion.5) | copy-start | bytes 6148
  11.0 24.3 %copy-start.32 = (f32[512]{0:T(512)}, f32[512]{0:T(512)S(1)}, u32[]{:S(2)}) copy-start(f32[512]{0:T(512)S(1)} %add_rsqrt_fusion.1) | copy-start | bytes 6148
  11.3 21.6 %copy-start.17 = (bf16[512,512]{1,0:T(8,128)(2,1)}, bf16[512,512]{1,0:T(8,128)(2,1)S(1)}, u32[]{:S(2)}) copy-start(bf16[512,512]{1,0:T(8,128)(2,1)S(1)} %slice.155) | copy-start | bytes 1572868
  12.8 34.2 %collective-permute-start.6 = (bf16[512,512]{0,1:T(8,128)(2,1)}, bf16[512,512]{0,1:T(8,128)(2,1)}, u32[]{:S(2)}, u32[]{:S(2)}) collective-permute-start(bf16[512,512]{0,1:T(8,128)(2,1)} %convolution_convert_fusion.7), channel_id=1, source_target_pairs={{0,3},{1,4},{2,5},{3,6},{4,7},{5,8},{6,9},{7,10},{8,11},{9,12},{10... | collective-permute-start | bytes 1572872 | tf_op jit(solution)/shard_map/ppermute | solution.py:23
  17.9 38.2 %collective-permute-start.7 = (bf16[512,512]{0,1:T(8,128)(2,1)}, bf16[512,512]{0,1:T(8,128)(2,1)}, u32[]{:S(2)}, u32[]{:S(2)}) collective-permute-start(bf16[512,512]{0,1:T(8,128)(2,1)} %convolution_convert_fusion.7), channel_id=1, source_target_pairs={{0,2},{1,3},{2,4},{3,5},{4,6},{5,7},{6,8},{7,9},{8,10},{9,11},{10,... | collective-permute-start | bytes 1572872 | tf_op jit(solution)/shard_map/ppermute | solution.py:23
  22.1 37.2 %collective-permute-start.8 = (bf16[512,512]{0,1:T(8,128)(2,1)}, bf16[512,512]{0,1:T(8,128)(2,1)}, u32[]{:S(2)}, u32[]{:S(2)}) collective-permute-start(bf16[512,512]{0,1:T(8,128)(2,1)} %convolution_convert_fusion.7), channel_id=1, source_target_pairs={{0,1},{1,2},{2,3},{3,4},{4,5},{5,6},{6,7},{7,8},{8,9},{9,10},{10,1... | collective-permute-start | bytes 1572872 | tf_op jit(solution)/shard_map/ppermute | solution.py:23
  24.4 48.5 %collective-permute-start.9 = (bf16[512,512]{0,1:T(8,128)(2,1)}, bf16[512,512]{0,1:T(8,128)(2,1)}, u32[]{:S(2)}, u32[]{:S(2)}) collective-permute-start(bf16[512,512]{0,1:T(8,128)(2,1)} %convolution_convert_fusion.7), channel_id=1, source_target_pairs={{1,0},{2,1},{3,2},{4,3},{5,4},{6,5},{7,6},{8,7},{9,8},{10,9},{11,1... | collective-permute-start | bytes 1572872 | tf_op jit(solution)/shard_map/ppermute | solution.py:23
  25.7 50.4 %collective-permute-start.10 = (bf16[512,512]{0,1:T(8,128)(2,1)}, bf16[512,512]{0,1:T(8,128)(2,1)}, u32[]{:S(2)}, u32[]{:S(2)}) collective-permute-start(bf16[512,512]{0,1:T(8,128)(2,1)} %convolution_convert_fusion.7), channel_id=1, source_target_pairs={{2,0},{3,1},{4,2},{5,3},{6,4},{7,5},{8,6},{9,7},{10,8},{11,9},{12,... | collective-permute-start | bytes 1572872 | tf_op jit(solution)/shard_map/ppermute | solution.py:23
  37.3 8.6 copy-start.12
  41.5 14.6 copy-start.25
  46.9 31.6 %collective-permute-start.11 = (bf16[512,512]{0,1:T(8,128)(2,1)}, bf16[512,512]{0,1:T(8,128)(2,1)S(1)}, u32[]{:S(2)}, u32[]{:S(2)}) collective-permute-start(bf16[512,512]{0,1:T(8,128)(2,1)} %convolution_convert_fusion.7), channel_id=1, source_target_pairs={{3,0},{4,1},{5,2},{6,3},{7,4},{8,5},{9,6},{10,7},{11,8},{12,9},{13... | collective-permute-start | bytes 1572872 | tf_op jit(solution)/shard_map/ppermute | solution.py:23
  56.1 112.6 %collective-permute-start = (bf16[512,512]{0,1:T(8,128)(2,1)S(1)}, bf16[512,512]{0,1:T(8,128)(2,1)}, u32[]{:S(2)}, u32[]{:S(2)}) collective-permute-start(bf16[512,512]{0,1:T(8,128)(2,1)S(1)} %copy-done.25), channel_id=1, source_target_pairs={{0,3},{1,4},{2,5},{3,6},{4,7},{5,8},{6,9},{7,10},{8,11},{9,12},{10... | collective-permute-start | bytes 1572872 | tf_op jit(solution)/shard_map/ppermute | solution.py:23
  59.3 112.1 %collective-permute-start.1 = (bf16[512,512]{0,1:T(8,128)(2,1)S(1)}, bf16[512,512]{0,1:T(8,128)(2,1)}, u32[]{:S(2)}, u32[]{:S(2)}) collective-permute-start(bf16[512,512]{0,1:T(8,128)(2,1)S(1)} %copy-done.25), channel_id=1, source_target_pairs={{0,2},{1,3},{2,4},{3,5},{4,6},{5,7},{6,8},{7,9},{8,10},{9,11},{10,... | collective-permute-start | bytes 1572872 | tf_op jit(solution)/shard_map/ppermute | solution.py:23
  72.9 99.5 %collective-permute-start.2 = (bf16[512,512]{0,1:T(8,128)(2,1)S(1)}, bf16[512,512]{0,1:T(8,128)(2,1)}, u32[]{:S(2)}, u32[]{:S(2)}) collective-permute-start(bf16[512,512]{0,1:T(8,128)(2,1)S(1)} %copy-done.25), channel_id=1, source_target_pairs={{0,1},{1,2},{2,3},{3,4},{4,5},{5,6},{6,7},{7,8},{8,9},{9,10},{10,1... | collective-permute-start | bytes 1572872 | tf_op jit(solution)/shard_map/ppermute | solution.py:23
  76.1 97.5 %collective-permute-start.3 = (bf16[512,512]{0,1:T(8,128)(2,1)S(1)}, bf16[512,512]{0,1:T(8,128)(2,1)}, u32[]{:S(2)}, u32[]{:S(2)}) collective-permute-start(bf16[512,512]{0,1:T(8,128)(2,1)S(1)} %copy-done.25), channel_id=1, source_target_pairs={{1,0},{2,1},{3,2},{4,3},{5,4},{6,5},{7,6},{8,7},{9,8},{10,9},{11,1... | collective-permute-start | bytes 1572872 | tf_op jit(solution)/shard_map/ppermute | solution.py:23
  78.5 96.2 %collective-permute-start.4 = (bf16[512,512]{0,1:T(8,128)(2,1)S(1)}, bf16[512,512]{0,1:T(8,128)(2,1)}, u32[]{:S(2)}, u32[]{:S(2)}) collective-permute-start(bf16[512,512]{0,1:T(8,128)(2,1)S(1)} %copy-done.25), channel_id=1, source_target_pairs={{2,0},{3,1},{4,2},{5,3},{6,4},{7,5},{8,6},{9,7},{10,8},{11,9},{12,... | collective-permute-start | bytes 1572872 | tf_op jit(solution)/shard_map/ppermute | solution.py:23
  168.8 11.9 collective-permute-start.5
  267.2 6.2 copy-start.1
  293.4 6.2 copy-start.1
  319.5 6.2 copy-start.1
  345.7 6.2 copy-start.1
  371.8 6.2 copy-start.1
  424.1 6.2 copy-start.1
  438.1 31.3 %copy-start.14 = (bf16[512,512]{1,0:T(8,128)(2,1)S(1)}, bf16[512,512]{1,0:T(8,128)(2,1)}, u32[]{:S(2)}) copy-start(bf16[512,512]{1,0:T(8,128)(2,1)} %param.14) | copy-start | bytes 1572868
  439.9 40.2 %collective-permute-start.23 = (bf16[512,8,64]{0,2,1:T(8,128)(2,1)}, bf16[512,8,64]{0,2,1:T(8,128)(2,1)}, u32[]{:S(2)}, u32[]{:S(2)}) collective-permute-start(bf16[512,8,64]{0,2,1:T(8,128)(2,1)} %get-tuple-element.446), channel_id=1, source_target_pairs={{0,3},{1,4},{2,5},{3,6},{4,7},{5,8},{6,9},{7,10},{8,11},{9,12},{10... | collective-permute-start | bytes 1572872 | tf_op jit(solution)/shard_map/ppermute | solution.py:23
  459.8 44.0 %collective-permute-start.22 = (bf16[512,8,64]{0,2,1:T(8,128)(2,1)}, bf16[512,8,64]{0,2,1:T(8,128)(2,1)}, u32[]{:S(2)}, u32[]{:S(2)}) collective-permute-start(bf16[512,8,64]{0,2,1:T(8,128)(2,1)} %get-tuple-element.447), channel_id=1, source_target_pairs={{0,2},{1,3},{2,4},{3,5},{4,6},{5,7},{6,8},{7,9},{8,10},{9,11},{10,... | collective-permute-start | bytes 1572872 | tf_op jit(solution)/shard_map/ppermute | solution.py:23
  469.6 45.0 %collective-permute-start.21 = (bf16[512,8,64]{0,2,1:T(8,128)(2,1)}, bf16[512,8,64]{0,2,1:T(8,128)(2,1)S(1)}, u32[]{:S(2)}, u32[]{:S(2)}) collective-permute-start(bf16[512,8,64]{0,2,1:T(8,128)(2,1)} %get-tuple-element.448), channel_id=1, source_target_pairs={{0,1},{1,2},{2,3},{3,4},{4,5},{5,6},{6,7},{7,8},{8,9},{9,10},{10,1... | collective-permute-start | bytes 1572872 | tf_op jit(solution)/shard_map/ppermute | solution.py:23
  471.9 44.9 %collective-permute-start.20 = (bf16[512,8,64]{0,2,1:T(8,128)(2,1)}, bf16[512,8,64]{0,2,1:T(8,128)(2,1)S(1)}, u32[]{:S(2)}, u32[]{:S(2)}) collective-permute-start(bf16[512,8,64]{0,2,1:T(8,128)(2,1)} %get-tuple-element.449), channel_id=1, source_target_pairs={{1,0},{2,1},{3,2},{4,3},{5,4},{6,5},{7,6},{8,7},{9,8},{10,9},{11,1... | collective-permute-start | bytes 1572872 | tf_op jit(solution)/shard_map/ppermute | solution.py:23
  473.2 46.4 %collective-permute-start.19 = (bf16[512,8,64]{0,2,1:T(8,128)(2,1)}, bf16[512,8,64]{0,2,1:T(8,128)(2,1)S(1)}, u32[]{:S(2)}, u32[]{:S(2)}) collective-permute-start(bf16[512,8,64]{0,2,1:T(8,128)(2,1)} %get-tuple-element.450), channel_id=1, source_target_pairs={{2,0},{3,1},{4,2},{5,3},{6,4},{7,5},{8,6},{9,7},{10,8},{11,9},{12,... | collective-permute-start | bytes 1572872 | tf_op jit(solution)/shard_map/ppermute | solution.py:23
  478.8 28.7 %copy-start.41 = (bf16[512,2048]{1,0:T(8,128)(2,1)S(1)}, bf16[512,2048]{1,0:T(8,128)(2,1)}, u32[]{:S(2)}) copy-start(bf16[512,2048]{1,0:T(8,128)(2,1)} %copy-done.40) | copy-start | bytes 6291460
  480.1 40.8 %collective-permute-start.18 = (bf16[512,8,64]{0,2,1:T(8,128)(2,1)S(1)}, bf16[512,8,64]{0,2,1:T(8,128)(2,1)S(1)}, u32[]{:S(2)}, u32[]{:S(2)}) collective-permute-start(bf16[512,8,64]{0,2,1:T(8,128)(2,1)S(1)} %copy-done.21), channel_id=1, source_target_pairs={{3,0},{4,1},{5,2},{6,3},{7,4},{8,5},{9,6},{10,7},{11,8},{12,9},{13... | collective-permute-start | bytes 1572872 | tf_op jit(solution)/shard_map/ppermute | solution.py:23
  503.8 18.4 %collective-permute-start.17 = (bf16[512,8,64]{0,2,1:T(8,128)(2,1)S(1)}, bf16[512,8,64]{0,2,1:T(8,128)(2,1)S(1)}, u32[]{:S(2)}, u32[]{:S(2)}) collective-permute-start(bf16[512,8,64]{0,2,1:T(8,128)(2,1)S(1)} %get-tuple-element.452), channel_id=1, source_target_pairs={{0,3},{1,4},{2,5},{3,6},{4,7},{5,8},{6,9},{7,10},{8,11},{9,12},{10... | collective-permute-start | bytes 1572872 | tf_op jit(solution)/shard_map/ppermute | solution.py:23
  514.6 11.1 copy-start.29
  514.6 11.1 copy-start.31
  514.6 11.1 copy-start.33
  514.6 11.1 copy-start.36
  514.6 14.3 collective-permute-start.16
  516.8 12.1 collective-permute-start.15
  519.6 9.4 collective-permute-start.14
  520.9 26.3 %collective-permute-start.13 = (bf16[512,8,64]{0,2,1:T(8,128)(2,1)S(1)}, bf16[512,8,64]{0,2,1:T(8,128)(2,1)S(1)}, u32[]{:S(2)}, u32[]{:S(2)}) collective-permute-start(bf16[512,8,64]{0,2,1:T(8,128)(2,1)S(1)} %get-tuple-element.456), channel_id=1, source_target_pairs={{2,0},{3,1},{4,2},{5,3},{6,4},{7,5},{8,6},{9,7},{10,8},{11,9},{12,... | collective-permute-start | bytes 1572872 | tf_op jit(solution)/shard_map/ppermute | solution.py:23
  522.2 26.3 %collective-permute-start.12 = (bf16[512,8,64]{0,2,1:T(8,128)(2,1)S(1)}, bf16[512,8,64]{0,2,1:T(8,128)(2,1)S(1)}, u32[]{:S(2)}, u32[]{:S(2)}) collective-permute-start(bf16[512,8,64]{0,2,1:T(8,128)(2,1)S(1)} %get-tuple-element.451), channel_id=1, source_target_pairs={{3,0},{4,1},{5,2},{6,3},{7,4},{8,5},{9,6},{10,7},{11,8},{12,9},{13... | collective-permute-start | bytes 1572872 | tf_op jit(solution)/shard_map/ppermute | solution.py:23
  526.7 24.9 %copy-start.18 = (bf16[512,512]{1,0:T(8,128)(2,1)S(1)}, bf16[512,512]{1,0:T(8,128)(2,1)}, u32[]{:S(2)}) copy-start(bf16[512,512]{1,0:T(8,128)(2,1)} %copy-done.17) | copy-start | bytes 1572868
  555.1 28.3 %copy-start.16 = (bf16[64,4,8,128]{3,1,2,0:T(4,128)(2,1)S(1)}, bf16[64,4,8,128]{3,1,2,0:T(4,128)(2,1)}, u32[]{:S(2)}) copy-start(bf16[64,4,8,128]{3,1,2,0:T(4,128)(2,1)} %copy.86) | copy-start | bytes 1572868
  657.3 628.1 %all-gather.6.cloned.1.call-start = ((), (), s32[]{:S(2)}) async-start(), calls=%async_computation | async-start | bytes 28366848 | tf_op jit(solution)/shard_map/all_gather | solution.py:318
  803.9 718.2 %all-gather.8.cloned.1.call-start = ((), (), s32[]{:S(2)}) async-start(), calls=%async_computation.1 | async-start | bytes 15759360 | tf_op jit(solution)/shard_map/all_gather | solution.py:330
  (33 other events, 104.3 us)
Sparse Core Ops, SparseCore 0:
  657.4 140.9 all-reduce.2
  804.0 481.3 all-gather.5
  1440.4 81.7 all-gather.7
